TPU v7x, 32 devices: a whole 2x2x4 slice. The times are simulated.
32 devices in a mesh: gx: 2 (over x), gy: 4 (over z), gz: 4 (over y, core).
Axes of the slice: x: 2, y: 2, z: 4, core: 2. Of those that a mesh axis runs over, the one named last changes fastest.
Arguments:
- displacement: bfloat16 [3, 8, 128, 64], P(None, 'gx', 'gy', 'gz'), may hold values from -6 to 6
- lift_weight: bfloat16 [27, 64, 3], replicated, may hold values from -1 to 1
- encode_weight: bfloat16 [27, 64, 64], replicated, may hold values from -0.21875 to 0.21875
- downward_weight: bfloat16 [8, 128, 64], replicated, may hold values from -0.375 to 0.375
- middle_first: bfloat16 [27, 128, 128], replicated, may hold values from -0.15625 to 0.15625
- middle_second: bfloat16 [27, 128, 128], replicated, may hold values from -0.15625 to 0.15625
- up_weight: bfloat16 [8, 64, 128], replicated, may hold values from -0.75 to 0.75
- decode_weight: bfloat16 [27, 64, 128], replicated, may hold values from -0.15625 to 0.15625
- head_weight: bfloat16 [3, 64], replicated, may hold values from -1 to 1
Outputs:
- imitated: float32 [3, 8, 128, 64], P(None, 'gx', 'gy', 'gz')
All inputs are finite; a program needn't handle non-finite values.
Results may differ from a plain program's by a relative error of at most 0.0055.
Values may be sent and summed in bfloat16 or wider, within the bound.
A program may use at most 64 MiB of HBM per device.

v0:
```python
import functools

import jax
import jax.numpy as jnp
from jax import lax
from jax.experimental import pallas as pl
from jax.experimental.pallas import tpu as pltpu
from jax.sharding import PartitionSpec as P

AXES = ("gx", "gy", "gz")
MESH = pl.DeviceIdType.MESH
NT = (((1,), (1,)), ((), ()))
DIRS = [
    (dx, dy, dz) for dx in (-1, 0, 1) for dy in (-1, 0, 1) for dz in (-1, 0, 1)
    if (dx, dy, dz) != (0, 0, 0)
]
F32, BF16 = jnp.float32, jnp.bfloat16


def padded_by(cells, width):
    for axis, dim in (("gx", 1), ("gy", 2), ("gz", 3)):
        count = lax.axis_size(axis)
        head = lax.slice_in_dim(cells, 0, width, axis=dim)
        tail = lax.slice_in_dim(cells, cells.shape[dim] - width, cells.shape[dim], axis=dim)
        cells = jnp.concatenate(
            [
                lax.ppermute(tail, axis, [(i, (i + 1) % count) for i in range(count)]),
                cells,
                lax.ppermute(head, axis, [((i + 1) % count, i) for i in range(count)]),
            ],
            axis=dim,
        )
    return cells


def leaky(value):
    return jnp.maximum(value, 0.1 * value)


def rounded(value):
    return leaky(value).astype(BF16)


def dot(rows, weight):
    return lax.dot_general(rows, weight, NT, preferred_element_type=F32)


def neighbour(direction):
    return tuple(
        lax.rem(lax.axis_index(axis) + lax.axis_size(axis) + step, lax.axis_size(axis))
        for axis, step in zip(AXES, direction)
    )


def exchange(body, below, above, first, last, sends, recvs, zc):
    size_x, size_y = body.shape[0] - 2, body.shape[1] // zc - 2
    copies = []
    for number, (dx, dy, dz) in enumerate(DIRS):
        def span(step, size, offset):
            if step == 0:
                return (offset, size, 1)
            return (offset + size - 1, 1, 0) if step > 0 else (offset, 1, size + 1)

        if dz == 0:
            sx, nx, tx = span(dx, size_x, 1)
            sy, ny, ty = span(dy, size_y, 1)
            src = body.at[pl.ds(sx, nx), pl.ds(sy * zc, ny * zc)]
            dst = body.at[pl.ds(tx, nx), pl.ds(ty * zc, ny * zc)]
        else:
            sx, nx, tx = span(dx, size_x, 0)
            sy, ny, ty = span(dy, size_y, 0)
            src = (last if dz > 0 else first).at[pl.ds(sx, nx), pl.ds(sy, ny)]
            dst = (below if dz > 0 else above).at[pl.ds(tx, nx), pl.ds(ty, ny)]
        copies.append(
            pltpu.make_async_remote_copy(
                src_ref=src, dst_ref=dst, send_sem=sends.at[number], recv_sem=recvs.at[number],
                device_id=neighbour((dx, dy, dz)), device_id_type=MESH,
            )
        )
    for copy in copies:
        copy.start()
    return copies


def masks(rows, zc):
    row = lax.rem(lax.broadcasted_iota(jnp.int32, (rows, 128), 0), zc)
    return row == 0, row == zc - 1


def half_mask(rows):
    return lax.broadcasted_iota(jnp.int32, (rows, 128), 1) < 64


def spread(edge, zc):
    return jnp.broadcast_to(edge, (edge.shape[0], zc, 128)).reshape(edge.shape[0] * zc, 128)


def shifted(plane, below, above, zc):
    rows = plane.shape[0]
    start, end = masks(rows, zc)
    down = jnp.where(start, below, pltpu.roll(plane, 1, 0))
    up = jnp.where(end, above, pltpu.roll(plane, rows - 1, 0))
    return down, up


def fine_conv(plane, twin, weight, x0, group, size_y, zc):
    summed = None
    pairs = size_y // 2
    for a in range(3):
        parts = []
        for source in (plane, twin):
            halves = [[], []]
            for g in range(group):
                value = source[x0 + g + a, pl.ds(0, (size_y + 2) * zc), :]
                value = value.reshape(pairs + 1, 2, zc, 128)
                halves[0].append(value[:, 0])
                halves[1].append(value[:, 1])
            parts.append(halves)
        for b in range(4):
            cut = [
                jnp.concatenate(
                    [
                        v[b // 2 : b // 2 + pairs].reshape(pairs * zc, 128)
                        for v in halves[b % 2]
                    ],
                    axis=0,
                ).astype(BF16)
                for halves in parts
            ]
            term = dot(jnp.concatenate(cut, axis=1), weight[4 * a + b])
            summed = term if summed is None else summed + term
    return summed


def coarse_conv(body, low, high, weight, zc):
    size_x, rows = body.shape[0] - 2, body.shape[1] - 2 * zc
    summed = None
    for a in range(3):
        for b in range(3):
            lhs = jnp.concatenate(
                [
                    jnp.concatenate(
                        [ref[x + a, pl.ds(b * zc, rows), :] for x in range(size_x)], axis=0
                    ).astype(BF16)
                    for ref in (low, body, high)
                ],
                axis=1,
            )
            tap = 9 * a + 3 * b
            kernel = jnp.concatenate([weight[tap], weight[tap + 1], weight[tap + 2]], axis=1)
            term = dot(lhs, kernel)
            summed = term if summed is None else summed + term
    return summed


def unet(
    sizes,
    rows_ref, lift_ref, encode_hbm, downward_ref, first_hbm, second_hbm, up_ref,
    skip_hbm, wide_hbm, head_ref,
    out_ref,
    chunks, fp, fe, sp, se, up, ue, acc,
    s_below, s_above, s_first, s_last,
    coarse_bufs, middle_bufs, deep_bufs, low, high,
    encode_w, first_w, second_w, skip_w, wide_w,
    load_sems, send_sems, recv_sems,
):
    size_x, size_y, size_z, rows_y = sizes
    zc, yc, xc = size_z // 2, size_y // 2, size_x // 2
    loads = [
        pltpu.make_async_copy(src, dst, load_sems.at[i])
        for i, (src, dst) in enumerate(
            (
                (encode_hbm, encode_w), (first_hbm, first_w), (second_hbm, second_w),
                (skip_hbm, skip_w), (wide_hbm, wide_w),
            )
        )
    ]
    for load in loads:
        load.start()
    barrier = pltpu.get_barrier_semaphore()
    for direction in DIRS:
        pl.semaphore_signal(barrier, inc=1, device_id=neighbour(direction), device_id_type=MESH)

    lhs = rows_ref[...]
    base = lift_ref[...]
    for p in range(zc + 1):
        z_lo, z_hi = (2 * p, 2 * p + 1) if p < zc else (size_z, -1)
        kernel = jnp.concatenate(
            [
                base if z == -1 else pltpu.roll(base, 3 * (z + 1), 1)
                for z in (z_lo, z_hi)
            ],
            axis=0,
        ).astype(BF16)
        chunks[p] = rounded(dot(lhs, kernel)).astype(F32)
    half = half_mask(rows_y)
    for x in range(size_x + 2):
        span = pl.ds(x * rows_y, rows_y)
        for p in range(zc):
            fp[x, pl.ds(p, rows_y, stride=zc), :] = chunks[p, span, :]
            fe[x, pl.ds(p, rows_y, stride=zc), :] = jnp.where(
                half, chunks[p + 1, span, :], chunks[zc if p == 0 else p - 1, span, :]
            )

    c_body, c_below, c_above, c_first, c_last = coarse_bufs
    m_body, m_below, m_above, m_first, m_last = middle_bufs
    d_body, d_below, d_above, d_first, d_last = deep_bufs
    loads[0].wait()

    @pl.loop(0, xc)
    def _(x):
        skip = rounded(fine_conv(fp, fe, encode_w, 2 * x, 2, size_y, zc))
        half_rows = yc * zc
        coarse = None
        for g in range(2):
            part = skip[g * half_rows : (g + 1) * half_rows]
            term = dot(part, downward_ref[g])
            coarse = term if coarse is None else coarse + term
            wide = part.astype(F32)
            plane = jnp.stack(
                [wide[:, :128].reshape(yc, zc, 128), wide[:, 128:].reshape(yc, zc, 128)], axis=1
            ).reshape(size_y, zc, 128)
            sp[2 * x + g + 1, pl.ds(zc, size_y * zc), :] = plane.reshape(size_y * zc, 128)
            s_first[2 * x + g] = plane[:, 0:1, :]
            s_last[2 * x + g] = plane[:, zc - 1 : zc, :]
        coarse = rounded(coarse).astype(F32)
        c_body[x + 1, pl.ds(zc, half_rows), :] = coarse
        c_first[x] = coarse.reshape(yc, zc, 128)[:, 0:1, :]
        c_last[x] = coarse.reshape(yc, zc, 128)[:, zc - 1 : zc, :]

    pl.semaphore_wait(barrier, len(DIRS))
    coarse_copies = exchange(*coarse_bufs, send_sems.at[0], recv_sems.at[0], zc)
    skip_copies = exchange(
        sp, s_below, s_above, s_first, s_last, send_sems.at[1], recv_sems.at[1], zc
    )

    def coarse_layer(bufs, weight, result):
        body, below, above = bufs[:3]
        for x in range(xc + 2):
            down, upper = shifted(body[x], spread(below[x], zc), spread(above[x], zc), zc)
            low[x] = down
            high[x] = upper
        value = rounded(coarse_conv(body, low, high, weight, zc)).astype(F32)
        target, _, _, first, last = result
        for x in range(xc):
            part = value[x * yc * zc : (x + 1) * yc * zc]
            target[x + 1, pl.ds(zc, yc * zc), :] = part
            first[x] = part.reshape(yc, zc, 128)[:, 0:1, :]
            last[x] = part.reshape(yc, zc, 128)[:, zc - 1 : zc, :]

    for copy in coarse_copies:
        copy.wait_recv()
    loads[1].wait()
    coarse_layer(coarse_bufs, first_w, middle_bufs)
    middle_copies = exchange(*middle_bufs, send_sems.at[2], recv_sems.at[2], zc)

    for copy in middle_copies:
        copy.wait_recv()
    loads[2].wait()
    coarse_layer(middle_bufs, second_w, deep_bufs)
    deep_copies = exchange(*deep_bufs, send_sems.at[3], recv_sems.at[3], zc)

    for copy in skip_copies:
        copy.wait_recv()
    fine_half = half_mask((size_y + 2) * zc)

    @pl.loop(0, size_x + 2)
    def _(x):
        down, upper = shifted(sp[x], spread(s_below[x], zc), spread(s_above[x], zc), zc)
        se[x] = jnp.where(fine_half, upper, down)

    loads[3].wait()

    @pl.loop(0, xc)
    def _(x):
        acc[x] = fine_conv(sp, se, skip_w, 2 * x, 2, size_y, zc)

    for copy in deep_copies:
        copy.wait_recv()
    coarse_rows = (yc + 2) * zc
    _, coarse_end = masks(coarse_rows, zc)

    def interleaved(value):
        even = value[:, 128:].reshape(yc + 2, zc, 128)[: yc + 1]
        odd = value[:, :128].reshape(yc + 2, zc, 128)[1:]
        return jnp.stack([even, odd], axis=1).reshape((size_y + 2) * zc, 128)

    for x in range(size_x + 2):
        source, a = (x + 1) // 2, (x + 1) % 2
        kernel = jnp.concatenate([up_ref[2 * a], up_ref[2 * a + 1]], axis=0)
        edge_rows = jnp.where(
            coarse_end, spread(d_above[source], zc), spread(d_below[source], zc)
        )
        plane = interleaved(rounded(dot(d_body[source].astype(BF16), kernel)).astype(F32))
        edge = interleaved(rounded(dot(edge_rows.astype(BF16), kernel)).astype(F32))
        down, upper = shifted(plane, edge, edge, zc)
        up[x] = plane
        ue[x] = jnp.where(fine_half, upper, down)

    loads[4].wait()

    @pl.loop(0, xc)
    def _(x):
        joined = rounded(acc[x] + fine_conv(up, ue, wide_w, 2 * x, 2, size_y, zc))
        result = dot(head_ref[...], joined)
        out_ref[2 * x] = result[:, : yc * zc]
        out_ref[2 * x + 1] = result[:, yc * zc :]

    for copy in coarse_copies + skip_copies + middle_copies + deep_copies:
        copy.wait_send()


def fine_kernel(weight):
    taps = weight.reshape(3, 3, 3, weight.shape[1], weight.shape[2])
    zero = jnp.zeros_like(taps[:, :, 0])
    low = jnp.concatenate([taps[:, :, 1], taps[:, :, 2], zero, taps[:, :, 0]], axis=-1)
    high = jnp.concatenate([taps[:, :, 0], taps[:, :, 1], taps[:, :, 2], zero], axis=-1)
    pair = jnp.concatenate([low, high], axis=2)
    blank = jnp.zeros_like(pair[:, :1])
    wide = jnp.concatenate(
        [jnp.concatenate([pair, blank], axis=1), jnp.concatenate([blank, pair], axis=1)], axis=2
    )
    return wide.reshape(12, wide.shape[2], wide.shape[3])


def local(
    displacement, lift_weight, encode_weight, downward_weight, middle_first, middle_second,
    up_weight, decode_weight, head_weight,
):
    comps, size_x, size_y, size_z = displacement.shape
    c1, c2 = encode_weight.shape[1], middle_first.shape[1]
    xc, yc, zc = size_x // 2, size_y // 2, size_z // 2
    rows_y = -(-(size_y + 2) // 8) * 8

    padded = padded_by(displacement, 2)
    cells = jnp.transpose(padded, (1, 2, 3, 0)).reshape(size_x + 4, size_y + 4, -1)
    rows = jnp.concatenate(
        [
            cells[a : a + size_x + 2, b : b + size_y + 2]
            for a in range(3) for b in range(3)
        ],
        axis=-1,
    )
    depth = rows.shape[-1]
    lanes = -(-depth // 128) * 128
    rows = jnp.pad(rows, ((0, 0), (0, rows_y - size_y - 2), (0, lanes - depth)))
    rows = rows.reshape((size_x + 2) * rows_y, lanes)
    base = jnp.transpose(lift_weight.reshape(9, 3, c1, comps), (2, 0, 1, 3)).reshape(c1, 9, -1)
    base = jnp.pad(base, ((0, 0), (0, 0), (0, depth // 9 - base.shape[-1]))).reshape(c1, depth)
    base = jnp.pad(base, ((0, 0), (0, lanes - depth))).astype(F32)

    encode = fine_kernel(encode_weight)
    skip_w = fine_kernel(decode_weight[:, :, :c1])
    wide_w = fine_kernel(decode_weight[:, :, c1:])
    downward = jnp.transpose(downward_weight.reshape(2, 4, c2, c1), (0, 2, 1, 3)).reshape(
        2, c2, 4 * c1
    )
    up_w = up_weight.reshape(4, 2 * c1, c2)
    head = jnp.einsum("pq,ki->pkqi", jnp.eye(4, dtype=BF16), head_weight).reshape(
        4 * comps, 4 * c1
    )
    head = jnp.pad(head, ((0, 16 - 4 * comps), (0, 0)))

    def coarse_set():
        return [
            pltpu.VMEM((xc + 2, (yc + 2) * zc, 128), F32),
            pltpu.VMEM((xc + 2, yc + 2, 1, 128), F32),
            pltpu.VMEM((xc + 2, yc + 2, 1, 128), F32),
            pltpu.VMEM((xc, yc, 1, 128), F32),
            pltpu.VMEM((xc, yc, 1, 128), F32),
        ]

    fine = pltpu.VMEM((size_x + 2, (size_y + 2) * zc, 128), F32)
    first = pltpu.VMEM((size_x + 2, rows_y * zc, 128), F32)
    vmem, anywhere = pl.BlockSpec(memory_space=pltpu.VMEM), pl.BlockSpec(memory_space=pl.ANY)
    result = pl.pallas_call(
        functools.partial(unet, (size_x, size_y, size_z, rows_y)),
        out_shape=jax.ShapeDtypeStruct((size_x, 16, yc * zc), F32),
        in_specs=[
            vmem, vmem, anywhere, vmem, anywhere, anywhere, vmem, anywhere, anywhere, vmem
        ],
        out_specs=vmem,
        scratch_shapes=[
            pltpu.VMEM((zc + 1, (size_x + 2) * rows_y, 128), F32),
            first, first, fine, fine, fine, fine,
            pltpu.VMEM((xc, 2 * yc * zc, 4 * c1), F32),
            pltpu.VMEM((size_x + 2, size_y + 2, 1, 128), F32),
            pltpu.VMEM((size_x + 2, size_y + 2, 1, 128), F32),
            pltpu.VMEM((size_x, size_y, 1, 128), F32),
            pltpu.VMEM((size_x, size_y, 1, 128), F32),
            coarse_set(), coarse_set(), coarse_set(),
            pltpu.VMEM((xc + 2, (yc + 2) * zc, 128), F32),
            pltpu.VMEM((xc + 2, (yc + 2) * zc, 128), F32),
            pltpu.VMEM(encode.shape, BF16),
            pltpu.VMEM(middle_first.shape, BF16),
            pltpu.VMEM(middle_second.shape, BF16),
            pltpu.VMEM(skip_w.shape, BF16),
            pltpu.VMEM(wide_w.shape, BF16),
            pltpu.SemaphoreType.DMA((5,)),
            pltpu.SemaphoreType.DMA((4, len(DIRS))),
            pltpu.SemaphoreType.DMA((4, len(DIRS))),
        ],
        compiler_params=pltpu.CompilerParams(
            collective_id=0, has_side_effects=True, vmem_limit_bytes=40 * 2**20
        ),
    )(rows, base, encode, downward, middle_first, middle_second, up_w, skip_w, wide_w, head)
    head_out = result[:, : 4 * comps].reshape(size_x, 2, 2, comps, yc, zc)
    head_out = jnp.transpose(head_out, (3, 0, 4, 1, 5, 2)).reshape(displacement.shape)
    return displacement.astype(F32) + head_out


def solution(mesh):
    placed = (P(None, "gx", "gy", "gz"), P(), P(), P(), P(), P(), P(), P(), P())
    return jax.shard_map(
        local, mesh=mesh, in_specs=placed, out_specs=P(None, "gx", "gy", "gz"), check_vma=False
    )
```

profile of v0, /device:TPU:0, one launch (start us, length us, event | category | flops | bytes accessed | tf_op | source)
XLA Modules:
  0.0 83.3 jit_solution(16585711132852480602)
XLA Ops:
  0.8 3.0 %collective-permute-start = (bf16[3,2,32,16]{2,3,1,0:T(8,128)(2,1)S(1)}, bf16[3,2,32,16]{2,3,1,0:T(8,128)(2,1)S(1)}, u32[]{:S(2)}, u32[]{:S(2)}) collective-permute-start(bf16[3,2,32,16]{2,3,1,0:T(8,128)(2,1)S(1)} %get-tuple-element.32), channel_id=1, source_target_pairs={{0,16},{16,0},{1,17},{17,1},{2,18},{18,2},{3,19},{19,3},{4,20},{20... | collective-permute-start | bytes 18440 | tf_op jit(solution)/shard_map/ppermute | solution.py:27
  3.8 1.4 %fusion.16 = (bf16[27,64,64]{2,1,0:T(8,128)(2,1)S(1)}, bf16[27,64,64]{2,1,0:T(8,128)(2,1)S(1)}) fusion(bf16[27,64,128]{2,1,0:T(8,128)(2,1)} %param.16), kind=kLoop, calls=%fused_computation.44 | loop fusion | bytes 884736 | tf_op jit(solution)/shard_map/slice | solution.py:354
  8.8 2.1 %collective-permute-start.2 = (bf16[3,8,2,16]{2,3,1,0:T(8,128)(2,1)}, bf16[3,8,2,16]{2,3,1,0:T(8,128)(2,1)}, u32[]{:S(2)}, u32[]{:S(2)}) collective-permute-start(bf16[3,8,2,16]{2,3,1,0:T(8,128)(2,1)} %get-tuple-element.29), channel_id=1, source_target_pairs={{0,4},{4,8},{8,12},{12,0},{1,5},{5,9},{9,13},{13,1},{2,6},{6,10},{... | collective-permute-start | bytes 4616 | tf_op jit(solution)/shard_map/ppermute | solution.py:27
  10.8 2.0 %collective-permute-start.3 = (bf16[3,8,2,16]{2,3,1,0:T(8,128)(2,1)}, bf16[3,8,2,16]{2,3,1,0:T(8,128)(2,1)}, u32[]{:S(2)}, u32[]{:S(2)}) collective-permute-start(bf16[3,8,2,16]{2,3,1,0:T(8,128)(2,1)} %get-tuple-element.30), channel_id=1, source_target_pairs={{4,0},{8,4},{12,8},{0,12},{5,1},{9,5},{13,9},{1,13},{6,2},{10,6},{... | collective-permute-start | bytes 4616 | tf_op jit(solution)/shard_map/ppermute | solution.py:29
  12.9 1.3 %fusion.7 = bf16[3,4,256,256]{3,2,1,0:T(8,128)(2,1)} fusion(bf16[3,3,128,256]{3,2,1,0:T(8,128)(2,1)S(1)} %fusion.12), kind=kLoop, calls=%fused_computation.9 | loop fusion | flops 6291456 | bytes 2162688 | tf_op jit(solution)/shard_map/concatenate | solution.py:320
  15.1 1.7 %collective-permute-done.2 = bf16[3,8,2,16]{2,3,1,0:T(8,128)(2,1)} collective-permute-done((bf16[3,8,2,16]{2,3,1,0:T(8,128)(2,1)}, bf16[3,8,2,16]{2,3,1,0:T(8,128)(2,1)}, u32[]{:S(2)}, u32[]{:S(2)}) %collective-permute-start.2) | collective-permute-done | bytes 1568 | tf_op jit(solution)/shard_map/ppermute | solution.py:27
  17.0 1.6 %pad_maximum_fusion.8 = (bf16[3,8,36,2]{2,3,1,0:T(2,128)(2,1)}, bf16[3,8,36,2]{2,3,1,0:T(2,128)(2,1)}) fusion(bf16[3,8,2,16]{2,3,1,0:T(8,128)(2,1)} %collective-permute-done.3, bf16[3,8,32,16]{2,3,1,0:T(8,128)(2,1)S(1)} %constant_dynamic-update-slice_fusion, bf16[3,8,2,16]{2,3,1,0:T(8,128)(2,1)} %collective-permute-done.2), kind=kLoop, calls=%fused_computation.37 | loop fusion | flops 20736 | bytes 34560 | tf_op jit(solution)/shard_map/slice | solution.py:24
  18.6 1.7 %collective-permute-start.5 = (bf16[3,8,36,2]{2,3,1,0:T(2,128)(2,1)}, bf16[3,8,36,2]{2,3,1,0:T(2,128)(2,1)}, u32[]{:S(2)}, u32[]{:S(2)}) collective-permute-start(bf16[3,8,36,2]{2,3,1,0:T(2,128)(2,1)} %get-tuple-element.17), channel_id=1, source_target_pairs={{1,0},{2,1},{3,2},{0,3},{5,4},{6,5},{7,6},{4,7},{9,8},{10,9},{11,1... | collective-permute-start | bytes 10376 | tf_op jit(solution)/shard_map/ppermute | solution.py:29
  23.0 1.2 %maximum_bitcast_fusion = bf16[8,36,20,3]{1,2,0,3:T(8,128)(2,1)S(1)} fusion(bf16[3,8,36,2]{2,3,1,0:T(2,128)(2,1)} %collective-permute-done.5, bf16[3,8,2,16]{2,3,1,0:T(8,128)(2,1)} %collective-permute-done.3, bf16[3,8,32,16]{2,3,1,0:T(8,128)(2,1)S(1)} %constant_dynamic-update-slice_fusion, bf16[3,8,2,16]{2,3,1,0:T(8,128)(2,1)} %collective-permute-done.2, ...), kind=kLoop, calls=%fused_computation.32 | loop fusion | flops 172800 | bytes 69120 | tf_op jit(solution)/shard_map/transpose | solution.py:336
  24.2 1.3 %fusion.17 = (bf16[6,34,60]{1,0,2:T(8,128)(2,1)}, bf16[6,34,60]{1,0,2:T(8,128)(2,1)}, bf16[6,34,60]{1,0,2:T(8,128)(2,1)}, bf16[6,34,60]{1,0,2:T(8,128)(2,1)}, bf...) fusion(bf16[8,36,60]{1,0,2:T(8,128)(2,1)S(1)} %bitcast.72), kind=kLoop, calls=%fused_computation.45 | loop fusion | bytes 440640 | tf_op jit(solution)/shard_map/slice | solution.py:339
  26.6 1.7 %copy.68 = bf16[6,34,60]{2,1,0:T(8,128)(2,1)} copy(bf16[6,34,60]{1,0,2:T(8,128)(2,1)} %get-tuple-element.27) | data formatting | bytes 48960 | tf_op jit(solution)/shard_map/slice | solution.py:339
  28.3 1.7 %copy.69 = bf16[6,34,60]{2,1,0:T(8,128)(2,1)} copy(bf16[6,34,60]{1,0,2:T(8,128)(2,1)} %get-tuple-element.26) | data formatting | bytes 48960 | tf_op jit(solution)/shard_map/slice | solution.py:339
  29.9 1.7 %copy.70 = bf16[6,34,60]{2,1,0:T(8,128)(2,1)} copy(bf16[6,34,60]{1,0,2:T(8,128)(2,1)} %get-tuple-element.25) | data formatting | bytes 48960 | tf_op jit(solution)/shard_map/slice | solution.py:339
  31.6 1.7 %copy.71 = bf16[6,34,60]{2,1,0:T(8,128)(2,1)} copy(bf16[6,34,60]{1,0,2:T(8,128)(2,1)} %get-tuple-element.24) | data formatting | bytes 48960 | tf_op jit(solution)/shard_map/slice | solution.py:339
  33.3 1.7 %copy.72 = bf16[6,34,60]{2,1,0:T(8,128)(2,1)} copy(bf16[6,34,60]{1,0,2:T(8,128)(2,1)} %get-tuple-element.23) | data formatting | bytes 48960 | tf_op jit(solution)/shard_map/slice | solution.py:339
  35.0 1.7 %copy.73 = bf16[6,34,60]{2,1,0:T(8,128)(2,1)} copy(bf16[6,34,60]{1,0,2:T(8,128)(2,1)} %get-tuple-element.22) | data formatting | bytes 48960 | tf_op jit(solution)/shard_map/slice | solution.py:339
  36.6 1.7 %copy.74 = bf16[6,34,60]{2,1,0:T(8,128)(2,1)} copy(bf16[6,34,60]{1,0,2:T(8,128)(2,1)} %get-tuple-element.21) | data formatting | bytes 48960 | tf_op jit(solution)/shard_map/slice | solution.py:339
  38.3 1.7 %copy.75 = bf16[6,34,60]{2,1,0:T(8,128)(2,1)} copy(bf16[6,34,60]{1,0,2:T(8,128)(2,1)} %get-tuple-element.20) | data formatting | bytes 48960 | tf_op jit(solution)/shard_map/slice | solution.py:339
  40.0 2.0 %concatenate.69 = bf16[6,34,540]{2,1,0:T(8,128)(2,1)} concatenate(bf16[6,34,60]{2,1,0:T(8,128)(2,1)S(1)} %copy.67, bf16[6,34,60]{2,1,0:T(8,128)(2,1)} %copy.68, bf16[6,34,60]{2,1,0:T(8,128)(2,1)} %copy.69, bf16[6,34,60]{2,1,0:T(8,128)(2,1)} %copy.70, bf16[6,34,60]{2,1,0:T(8,128)(2,1)} %copy.71, bf16[6,34,60]{2,1,0:T(8,128)(2,1)} %copy.72, bf16[6,34,60]{2,1,0:T(8,128)(2,1)} %copy.73, ...), dimensions={2} | concatenate | bytes 440640 | tf_op jit(solution)/shard_map/concatenate | solution.py:337
  43.0 1.4 %copy-done = bf16[3,4,256,256]{3,2,1,0:T(8,128)(2,1)S(1)} copy-done((bf16[3,4,256,256]{3,2,1,0:T(8,128)(2,1)S(1)}, bf16[3,4,256,256]{3,2,1,0:T(8,128)(2,1)}, u32[]{:S(2)}) %copy-start) | copy-done | bytes 1572888
  44.4 1.2 %copy-done.1 = bf16[27,128,128]{2,1,0:T(8,128)(2,1)S(1)} copy-done((bf16[27,128,128]{2,1,0:T(8,128)(2,1)S(1)}, bf16[27,128,128]{2,1,0:T(8,128)(2,1)}, u32[]{:S(2)}) %copy-start.1) | copy-done | bytes 884760
  45.6 1.2 %copy-done.2 = bf16[27,128,128]{2,1,0:T(8,128)(2,1)S(1)} copy-done((bf16[27,128,128]{2,1,0:T(8,128)(2,1)S(1)}, bf16[27,128,128]{2,1,0:T(8,128)(2,1)}, u32[]{:S(2)}) %copy-start.2) | copy-done | bytes 884760
  47.7 32.9 %shard_map.91 = f32[4,16,128]{2,1,0:T(8,128)S(1)} custom-call(bf16[240,640]{1,0:T(8,128)(2,1)S(1)} %bitcast.69, f32[64,640]{1,0:T(8,128)S(1)} %pad_convert_fusion.lift_ref, bf16[12,256,256]{2,1,0:T(8,128)(2,1)S(1)} %bitcast.66, bf16[2,128,256]{2,1,0:T(8,128)(2,1)S(1)} %copy.87.downward_ref, bf16[27,128,128]{2,1,0:T(8,128)(2,1)S(1)} %copy-done.1, ...), custom_call_target="tpu_custom_call" | custom-call | tf_op jit(solution)/shard_map/pallas_call | solution.py:376
  80.9 1.3 %copy.89 = f32[3,4,16,2,8,2]{1,5,4,3,2,0:T(2,128)S(1)} copy(f32[3,4,16,2,8,2]{4,2,1,0,5,3:T(8,128)S(1)} %bitcast.76) | data formatting | bytes 49152 | tf_op jit(solution)/shard_map/transpose | solution.py:408
  (52 shorter events, 12.3 us)
Async XLA Ops:
  0.8 7.2 %collective-permute-start = (bf16[3,2,32,16]{2,3,1,0:T(8,128)(2,1)S(1)}, bf16[3,2,32,16]{2,3,1,0:T(8,128)(2,1)S(1)}, u32[]{:S(2)}, u32[]{:S(2)}) collective-permute-start(bf16[3,2,32,16]{2,3,1,0:T(8,128)(2,1)S(1)} %get-tuple-element.32), channel_id=1, source_target_pairs={{0,16},{16,0},{1,17},{17,1},{2,18},{18,2},{3,19},{19,3},{4,20},{20... | collective-permute-start | bytes 18440 | tf_op jit(solution)/shard_map/ppermute | solution.py:27
  3.7 4.3 %collective-permute-start.1 = (bf16[3,2,32,16]{2,3,1,0:T(8,128)(2,1)S(1)}, bf16[3,2,32,16]{2,3,1,0:T(8,128)(2,1)S(1)}, u32[]{:S(2)}, u32[]{:S(2)}) collective-permute-start(bf16[3,2,32,16]{2,3,1,0:T(8,128)(2,1)S(1)} %get-tuple-element.31), channel_id=1, source_target_pairs={{16,0},{0,16},{17,1},{1,17},{18,2},{2,18},{19,3},{3,19},{20,4},{4,... | collective-permute-start | bytes 18440 | tf_op jit(solution)/shard_map/ppermute | solution.py:29
  3.8 1.5 %copy-start.4 = (bf16[27,64,64]{2,1,0:T(8,128)(2,1)S(1)}, bf16[27,64,64]{2,1,0:T(8,128)(2,1)}, u32[]{:S(2)}) copy-start(bf16[27,64,64]{2,1,0:T(8,128)(2,1)} %param.11) | copy-start | bytes 663556
  6.2 0.7 copy-start.8
  6.9 1.1 %copy-start.5 = (bf16[3,4,32,16]{2,3,1,0:T(8,128)(2,1)S(1)}, bf16[3,4,32,16]{2,3,1,0:T(8,128)(2,1)}, u32[]{:S(2)}) copy-start(bf16[3,4,32,16]{2,3,1,0:T(8,128)(2,1)} %param.9) | copy-start | bytes 36868
  8.8 5.4 %copy-start.7 = (bf16[27,64,3]{1,0,2:T(8,128)(2,1)S(1)}, bf16[27,64,3]{1,0,2:T(8,128)(2,1)}, u32[]{:S(2)}) copy-start(bf16[27,64,3]{1,0,2:T(8,128)(2,1)} %param.10) | copy-start | bytes 31108
  8.8 8.0 %collective-permute-start.2 = (bf16[3,8,2,16]{2,3,1,0:T(8,128)(2,1)}, bf16[3,8,2,16]{2,3,1,0:T(8,128)(2,1)}, u32[]{:S(2)}, u32[]{:S(2)}) collective-permute-start(bf16[3,8,2,16]{2,3,1,0:T(8,128)(2,1)} %get-tuple-element.29), channel_id=1, source_target_pairs={{0,4},{4,8},{8,12},{12,0},{1,5},{5,9},{9,13},{13,1},{2,6},{6,10},{... | collective-permute-start | bytes 4616 | tf_op jit(solution)/shard_map/ppermute | solution.py:27
  10.8 6.1 %collective-permute-start.3 = (bf16[3,8,2,16]{2,3,1,0:T(8,128)(2,1)}, bf16[3,8,2,16]{2,3,1,0:T(8,128)(2,1)}, u32[]{:S(2)}, u32[]{:S(2)}) collective-permute-start(bf16[3,8,2,16]{2,3,1,0:T(8,128)(2,1)} %get-tuple-element.30), channel_id=1, source_target_pairs={{4,0},{8,4},{12,8},{0,12},{5,1},{9,5},{13,9},{1,13},{6,2},{10,6},{... | collective-permute-start | bytes 4616 | tf_op jit(solution)/shard_map/ppermute | solution.py:29
  18.6 4.5 %collective-permute-start.4 = (bf16[3,8,36,2]{2,3,1,0:T(2,128)(2,1)}, bf16[3,8,36,2]{2,3,1,0:T(2,128)(2,1)}, u32[]{:S(2)}, u32[]{:S(2)}) collective-permute-start(bf16[3,8,36,2]{2,3,1,0:T(2,128)(2,1)} %get-tuple-element.16), channel_id=1, source_target_pairs={{0,1},{1,2},{2,3},{3,0},{4,5},{5,6},{6,7},{7,4},{8,9},{9,10},{10,1... | collective-permute-start | bytes 10376 | tf_op jit(solution)/shard_map/ppermute | solution.py:27
  18.6 4.5 %collective-permute-start.5 = (bf16[3,8,36,2]{2,3,1,0:T(2,128)(2,1)}, bf16[3,8,36,2]{2,3,1,0:T(2,128)(2,1)}, u32[]{:S(2)}, u32[]{:S(2)}) collective-permute-start(bf16[3,8,36,2]{2,3,1,0:T(2,128)(2,1)} %get-tuple-element.17), channel_id=1, source_target_pairs={{1,0},{2,1},{3,2},{0,3},{5,4},{6,5},{7,6},{4,7},{9,8},{10,9},{11,1... | collective-permute-start | bytes 10376 | tf_op jit(solution)/shard_map/ppermute | solution.py:29
  43.0 1.4 %copy-start = (bf16[3,4,256,256]{3,2,1,0:T(8,128)(2,1)S(1)}, bf16[3,4,256,256]{3,2,1,0:T(8,128)(2,1)}, u32[]{:S(2)}) copy-start(bf16[3,4,256,256]{3,2,1,0:T(8,128)(2,1)} %fusion.7) | copy-start | bytes 4718596
  44.4 1.2 %copy-start.1 = (bf16[27,128,128]{2,1,0:T(8,128)(2,1)S(1)}, bf16[27,128,128]{2,1,0:T(8,128)(2,1)}, u32[]{:S(2)}) copy-start(bf16[27,128,128]{2,1,0:T(8,128)(2,1)} %first_hbm.1) | copy-start | bytes 2654212
  45.6 1.2 %copy-start.2 = (bf16[27,128,128]{2,1,0:T(8,128)(2,1)S(1)}, bf16[27,128,128]{2,1,0:T(8,128)(2,1)}, u32[]{:S(2)}) copy-start(bf16[27,128,128]{2,1,0:T(8,128)(2,1)} %second_hbm.1) | copy-start | bytes 2654212
  46.8 0.9 %copy-start.3 = (bf16[8,64,128]{2,1,0:T(8,128)(2,1)S(1)}, bf16[8,64,128]{2,1,0:T(8,128)(2,1)}, u32[]{:S(2)}) copy-start(bf16[8,64,128]{2,1,0:T(8,128)(2,1)} %param.15) | copy-start | bytes 393220
  80.6 2.0 %copy-start.6 = (bf16[3,4,32,16]{2,3,1,0:T(8,128)(2,1)S(1)}, bf16[3,4,32,16]{2,3,1,0:T(8,128)(2,1)}, u32[]{:S(2)}) copy-start(bf16[3,4,32,16]{2,3,1,0:T(8,128)(2,1)} %param.9) | copy-start | bytes 36868
where the time goes:
time: 84.1 us; the launch traced here: 83.3 us
  Pallas kernels  32.9 us (39%)
  local copies, waits for them, and re-layouts  31.4 us (37%)
  starting transfers between devices  8.85 us (11%)
  other arithmetic  7.94 us (9%)
  waiting for transfers between devices  1.9 us (2%)
    pallas_call x1, Pallas kernels, local(): pl.pallas_call(functools.partial(unet, (size_x, size_y, size_z, rows_y)),...  32.9 us
    slice x10, local copies, waits for them, and re-layouts, local(): cells[a:a + size_x + 2, b:b + size_y + 2]  15.7 us
    ppermute x3, starting transfers between devices, padded_by(): lax.ppermute(tail, axis, [(i, (i + 1) % count) for i in range(count)])  5.03 us
    unnamed x20, local copies, waits for them, and re-layouts  4.92 us
    ppermute x3, starting transfers between devices, padded_by(): lax.ppermute(head, axis, [((i + 1) % count, i) for i in range(count)])  3.83 us
    concatenate x1, local copies, waits for them, and re-layouts, local(): jnp.concatenate([cells[a:a + size_x + 2, b:b + size_y + 2] for a in range...  2.03 us
    ppermute x3, waiting for transfers between devices, padded_by(): lax.ppermute(tail, axis, [(i, (i + 1) % count) for i in range(count)])  1.72 us
    concatenate x2, other arithmetic, fine_kernel(): jnp.concatenate([jnp.concatenate([pair, blank], axis=1), jnp.concatenate(...  1.72 us
  transfers between devices with their start and end apart: 6, of which 2 were waited for; matrix products, arithmetic and copies ran while one was open for 10% of the time, Pallas kernels for 0%

commit v1 on v0

--- a/solution.py
+++ b/solution.py
@@ -15,22 +15,7 @@
     if (dx, dy, dz) != (0, 0, 0)
 ]
 F32, BF16 = jnp.float32, jnp.bfloat16
-
-
-def padded_by(cells, width):
-    for axis, dim in (("gx", 1), ("gy", 2), ("gz", 3)):
-        count = lax.axis_size(axis)
-        head = lax.slice_in_dim(cells, 0, width, axis=dim)
-        tail = lax.slice_in_dim(cells, cells.shape[dim] - width, cells.shape[dim], axis=dim)
-        cells = jnp.concatenate(
-            [
-                lax.ppermute(tail, axis, [(i, (i + 1) % count) for i in range(count)]),
-                cells,
-                lax.ppermute(head, axis, [((i + 1) % count, i) for i in range(count)]),
-            ],
-            axis=dim,
-        )
-    return cells
+RIM = 16
 
 
 def leaky(value):
@@ -80,6 +65,43 @@
     for copy in copies:
         copy.start()
     return copies
+
+
+def send_cells(cells, block, sends, recvs):
+    size_x, size_y = cells.shape[:2]
+    copies = []
+    for number, (dx, dy, dz) in enumerate(DIRS):
+        sx, nx, tx = {0: (0, size_x, 2), 1: (size_x - 2, 2, 0), -1: (0, 2, size_x + 2)}[dx]
+        sy, ny, ty = {
+            0: (0, size_y, RIM), 1: (size_y - RIM, RIM, 0), -1: (0, RIM, size_y + RIM)
+        }[dy]
+        copies.append(
+            pltpu.make_async_remote_copy(
+                src_ref=cells.at[pl.ds(sx, nx), pl.ds(sy, ny)],
+                dst_ref=block.at[1 - dz, pl.ds(tx, nx), pl.ds(ty, ny)],
+                send_sem=sends.at[number], recv_sem=recvs.at[number],
+                device_id=neighbour((dx, dy, dz)), device_id_type=MESH,
+            )
+        )
+    for copy in copies:
+        copy.start()
+    return copies
+
+
+def build_fine(raw, wide, lo, hi):
+    out = raw.shape[1]
+    blank = jnp.zeros((2 * out, wide.shape[2]), BF16)
+    zero = jnp.zeros((out, hi - lo), BF16)
+    for a in range(3):
+        wide[4 * a, 2 * out :, :] = blank
+        wide[4 * a + 3, : 2 * out, :] = blank
+        for b in range(3):
+            taps = [raw[9 * a + 3 * b + c][:, lo:hi] for c in range(3)]
+            low = jnp.concatenate([taps[1], taps[2], zero, taps[0]], axis=1)
+            high = jnp.concatenate([taps[0], taps[1], taps[2], zero], axis=1)
+            pair = jnp.concatenate([low, high], axis=0)
+            wide[4 * a + b, : 2 * out, :] = pair
+            wide[4 * a + b + 1, 2 * out :, :] = pair
 
 
 def masks(rows, zc):
@@ -155,23 +177,24 @@
 
 def unet(
     sizes,
-    rows_ref, lift_ref, encode_hbm, downward_ref, first_hbm, second_hbm, up_ref,
-    skip_hbm, wide_hbm, head_ref,
+    cells_ref, lift_ref, encode_hbm, downward_hbm, first_hbm, second_hbm, up_hbm,
+    decode_hbm, head_ref,
     out_ref,
-    chunks, fp, fe, sp, se, up, ue, acc,
+    block, joint, lhs32, lhs16, chunks, fp, fe, sp, se, up, ue, acc,
     s_below, s_above, s_first, s_last,
     coarse_bufs, middle_bufs, deep_bufs, low, high,
-    encode_w, first_w, second_w, skip_w, wide_w,
+    encode_raw, downward_raw, first_w, second_w, up_ref, decode_raw,
+    encode_w, skip_w, wide_w,
     load_sems, send_sems, recv_sems,
 ):
-    size_x, size_y, size_z, rows_y = sizes
+    comps, size_x, size_y, size_z, rows_y = sizes
     zc, yc, xc = size_z // 2, size_y // 2, size_x // 2
     loads = [
         pltpu.make_async_copy(src, dst, load_sems.at[i])
         for i, (src, dst) in enumerate(
             (
-                (encode_hbm, encode_w), (first_hbm, first_w), (second_hbm, second_w),
-                (skip_hbm, skip_w), (wide_hbm, wide_w),
+                (encode_hbm, encode_raw), (downward_hbm, downward_raw), (first_hbm, first_w),
+                (decode_hbm, decode_raw), (second_hbm, second_w), (up_hbm, up_ref),
             )
         )
     ]
@@ -180,20 +203,67 @@
     barrier = pltpu.get_barrier_semaphore()
     for direction in DIRS:
         pl.semaphore_signal(barrier, inc=1, device_id=neighbour(direction), device_id_type=MESH)
-
-    lhs = rows_ref[...]
-    base = lift_ref[...]
+    pl.semaphore_wait(barrier, len(DIRS))
+    cell_copies = send_cells(cells_ref, block, send_sems.at[4], recv_sems.at[4])
+    block[1, pl.ds(2, size_x), pl.ds(RIM, size_y), :] = cells_ref[...]
+
+    groups = []
+    for g in range(5):
+        total = None
+        for tap in range(2 * g, min(2 * g + 2, 9)):
+            for c in range(3):
+                piece = lift_ref[3 * tap + c].astype(F32)
+                shift = 64 * (tap % 2) + comps * c
+                piece = pltpu.roll(piece, shift, 1) if shift else piece
+                total = piece if total is None else total + piece
+        groups.append(total)
+    loads[0].wait()
+    build_fine(encode_raw, encode_w, 0, encode_raw.shape[2])
+    loads[1].wait()
+    downward = [
+        jnp.concatenate([downward_raw[4 * a + t] for t in range(4)], axis=1) for a in range(2)
+    ]
+    for copy in cell_copies:
+        copy.wait_recv()
+
+    width = comps * size_z
+    edge = 2 * comps
+    all_rows = size_y + 2 * RIM
+    lane = lax.broadcasted_iota(jnp.int32, (all_rows, 128), 1)
+    for x in range(size_x + 4):
+        own = pltpu.roll(block[1, x].astype(F32), edge, 1)
+        before = pltpu.roll(block[0, x].astype(F32), 128 - (width - edge), 1)
+        after = pltpu.roll(block[2, x].astype(F32), width + edge, 1)
+        joint[x] = jnp.where(
+            lane < edge,
+            before,
+            jnp.where(lane < edge + width, own, jnp.where(lane < width + 2 * edge, after, 0.0)),
+        )
+    half = half_mask(rows_y)
+    for x in range(size_x + 2):
+        for g in range(5):
+            parts = [
+                joint[x + tap // 3, pl.ds(RIM - 2 + tap % 3, rows_y), :]
+                for tap in range(2 * g, min(2 * g + 2, 9))
+            ]
+            other = pltpu.roll(parts[1], 64, 1) if len(parts) > 1 else jnp.zeros_like(parts[0])
+            lhs32[pl.ds(x * rows_y, rows_y), 128 * g : 128 * g + 128] = jnp.where(
+                half, parts[0], other
+            )
+    lhs16[...] = lhs32[...].astype(BF16)
+
     for p in range(zc + 1):
         z_lo, z_hi = (2 * p, 2 * p + 1) if p < zc else (size_z, -1)
         kernel = jnp.concatenate(
             [
-                base if z == -1 else pltpu.roll(base, 3 * (z + 1), 1)
+                jnp.concatenate(
+                    [pltpu.roll(v, comps * (z + 1), 1) if z + 1 else v for v in groups], axis=1
+                )
                 for z in (z_lo, z_hi)
             ],
             axis=0,
         ).astype(BF16)
-        chunks[p] = rounded(dot(lhs, kernel)).astype(F32)
-    half = half_mask(rows_y)
+        chunks[p] = rounded(dot(lhs16[...], kernel)).astype(F32)
     for x in range(size_x + 2):
         span = pl.ds(x * rows_y, rows_y)
         for p in range(zc):
@@ -205,7 +275,6 @@
     c_body, c_below, c_above, c_first, c_last = coarse_bufs
     m_body, m_below, m_above, m_first, m_last = middle_bufs
     d_body, d_below, d_above, d_first, d_last = deep_bufs
-    loads[0].wait()
 
     @pl.loop(0, xc)
     def _(x):
@@ -214,7 +283,7 @@
         coarse = None
         for g in range(2):
             part = skip[g * half_rows : (g + 1) * half_rows]
-            term = dot(part, downward_ref[g])
+            term = dot(part, downward[g])
             coarse = term if coarse is None else coarse + term
             wide = part.astype(F32)
             plane = jnp.stack(
@@ -228,7 +297,6 @@
         c_first[x] = coarse.reshape(yc, zc, 128)[:, 0:1, :]
         c_last[x] = coarse.reshape(yc, zc, 128)[:, zc - 1 : zc, :]
 
-    pl.semaphore_wait(barrier, len(DIRS))
     coarse_copies = exchange(*coarse_bufs, send_sems.at[0], recv_sems.at[0], zc)
     skip_copies = exchange(
         sp, s_below, s_above, s_first, s_last, send_sems.at[1], recv_sems.at[1], zc
@@ -248,15 +316,19 @@
             first[x] = part.reshape(yc, zc, 128)[:, 0:1, :]
             last[x] = part.reshape(yc, zc, 128)[:, zc - 1 : zc, :]
 
+    loads[2].wait()
+    loads[3].wait()
+    channels = decode_raw.shape[2] // 2
+    build_fine(decode_raw, skip_w, 0, channels)
+    build_fine(decode_raw, wide_w, channels, 2 * channels)
     for copy in coarse_copies:
         copy.wait_recv()
-    loads[1].wait()
     coarse_layer(coarse_bufs, first_w, middle_bufs)
     middle_copies = exchange(*middle_bufs, send_sems.at[2], recv_sems.at[2], zc)
 
     for copy in middle_copies:
         copy.wait_recv()
-    loads[2].wait()
+    loads[4].wait()
     coarse_layer(middle_bufs, second_w, deep_bufs)
     deep_copies = exchange(*deep_bufs, send_sems.at[3], recv_sems.at[3], zc)
 
@@ -269,7 +341,7 @@
         down, upper = shifted(sp[x], spread(s_below[x], zc), spread(s_above[x], zc), zc)
         se[x] = jnp.where(fine_half, upper, down)
 
-    loads[3].wait()
+    loads[5].wait()
 
     @pl.loop(0, xc)
     def _(x):
@@ -297,8 +369,6 @@
         up[x] = plane
         ue[x] = jnp.where(fine_half, upper, down)
 
-    loads[4].wait()
-
     @pl.loop(0, xc)
     def _(x):
         joined = rounded(acc[x] + fine_conv(up, ue, wide_w, 2 * x, 2, size_y, zc))
@@ -306,21 +376,8 @@
         out_ref[2 * x] = result[:, : yc * zc]
         out_ref[2 * x + 1] = result[:, yc * zc :]
 
-    for copy in coarse_copies + skip_copies + middle_copies + deep_copies:
+    for copy in cell_copies + coarse_copies + skip_copies + middle_copies + deep_copies:
         copy.wait_send()
-
-
-def fine_kernel(weight):
-    taps = weight.reshape(3, 3, 3, weight.shape[1], weight.shape[2])
-    zero = jnp.zeros_like(taps[:, :, 0])
-    low = jnp.concatenate([taps[:, :, 1], taps[:, :, 2], zero, taps[:, :, 0]], axis=-1)
-    high = jnp.concatenate([taps[:, :, 0], taps[:, :, 1], taps[:, :, 2], zero], axis=-1)
-    pair = jnp.concatenate([low, high], axis=2)
-    blank = jnp.zeros_like(pair[:, :1])
-    wide = jnp.concatenate(
-        [jnp.concatenate([pair, blank], axis=1), jnp.concatenate([blank, pair], axis=1)], axis=2
-    )
-    return wide.reshape(12, wide.shape[2], wide.shape[3])
 
 
 def local(
@@ -332,29 +389,9 @@
     xc, yc, zc = size_x // 2, size_y // 2, size_z // 2
     rows_y = -(-(size_y + 2) // 8) * 8
 
-    padded = padded_by(displacement, 2)
-    cells = jnp.transpose(padded, (1, 2, 3, 0)).reshape(size_x + 4, size_y + 4, -1)
-    rows = jnp.concatenate(
-        [
-            cells[a : a + size_x + 2, b : b + size_y + 2]
-            for a in range(3) for b in range(3)
-        ],
-        axis=-1,
-    )
-    depth = rows.shape[-1]
-    lanes = -(-depth // 128) * 128
-    rows = jnp.pad(rows, ((0, 0), (0, rows_y - size_y - 2), (0, lanes - depth)))
-    rows = rows.reshape((size_x + 2) * rows_y, lanes)
-    base = jnp.transpose(lift_weight.reshape(9, 3, c1, comps), (2, 0, 1, 3)).reshape(c1, 9, -1)
-    base = jnp.pad(base, ((0, 0), (0, 0), (0, depth // 9 - base.shape[-1]))).reshape(c1, depth)
-    base = jnp.pad(base, ((0, 0), (0, lanes - depth))).astype(F32)
-
-    encode = fine_kernel(encode_weight)
-    skip_w = fine_kernel(decode_weight[:, :, :c1])
-    wide_w = fine_kernel(decode_weight[:, :, c1:])
-    downward = jnp.transpose(downward_weight.reshape(2, 4, c2, c1), (0, 2, 1, 3)).reshape(
-        2, c2, 4 * c1
-    )
+    cells = jnp.transpose(displacement, (1, 2, 3, 0)).reshape(size_x, size_y, -1)
+    cells = jnp.pad(cells, ((0, 0), (0, 0), (0, 128 - cells.shape[-1])))
+    lift = jnp.pad(lift_weight, ((0, 0), (0, 0), (0, 128 - comps)))
     up_w = up_weight.reshape(4, 2 * c1, c2)
     head = jnp.einsum("pq,ki->pkqi", jnp.eye(4, dtype=BF16), head_weight).reshape(
         4 * comps, 4 * c1
@@ -372,15 +409,17 @@
 
     fine = pltpu.VMEM((size_x + 2, (size_y + 2) * zc, 128), F32)
     first = pltpu.VMEM((size_x + 2, rows_y * zc, 128), F32)
-    vmem, anywhere = pl.BlockSpec(memory_space=pltpu.VMEM), pl.BlockSpec(memory_space=pl.ANY)
+    vmem, anywhere = pl.BlockSpec(memory_space=pltpu.VMEM), pl.BlockSpec(memory_space=pltpu.HBM)
     result = pl.pallas_call(
-        functools.partial(unet, (size_x, size_y, size_z, rows_y)),
+        functools.partial(unet, (comps, size_x, size_y, size_z, rows_y)),
         out_shape=jax.ShapeDtypeStruct((size_x, 16, yc * zc), F32),
-        in_specs=[
-            vmem, vmem, anywhere, vmem, anywhere, anywhere, vmem, anywhere, anywhere, vmem
-        ],
+        in_specs=[vmem, vmem] + [anywhere] * 6 + [vmem],
         out_specs=vmem,
         scratch_shapes=[
+            pltpu.VMEM((3, size_x + 4, size_y + 2 * RIM, 128), BF16),
+            pltpu.VMEM((size_x + 4, size_y + 2 * RIM, 128), F32),
+            pltpu.VMEM(((size_x + 2) * rows_y, 640), F32),
+            pltpu.VMEM(((size_x + 2) * rows_y, 640), BF16),
             pltpu.VMEM((zc + 1, (size_x + 2) * rows_y, 128), F32),
             first, first, fine, fine, fine, fine,
             pltpu.VMEM((xc, 2 * yc * zc, 4 * c1), F32),
@@ -391,19 +430,26 @@
             coarse_set(), coarse_set(), coarse_set(),
             pltpu.VMEM((xc + 2, (yc + 2) * zc, 128), F32),
             pltpu.VMEM((xc + 2, (yc + 2) * zc, 128), F32),
-            pltpu.VMEM(encode.shape, BF16),
+            pltpu.VMEM(encode_weight.shape, BF16),
+            pltpu.VMEM(downward_weight.shape, BF16),
             pltpu.VMEM(middle_first.shape, BF16),
             pltpu.VMEM(middle_second.shape, BF16),
-            pltpu.VMEM(skip_w.shape, BF16),
-            pltpu.VMEM(wide_w.shape, BF16),
-            pltpu.SemaphoreType.DMA((5,)),
-            pltpu.SemaphoreType.DMA((4, len(DIRS))),
-            pltpu.SemaphoreType.DMA((4, len(DIRS))),
+            pltpu.VMEM(up_w.shape, BF16),
+            pltpu.VMEM(decode_weight.shape, BF16),
+            pltpu.VMEM((12, 4 * c1, 4 * c1), BF16),
+            pltpu.VMEM((12, 4 * c1, 4 * c1), BF16),
+            pltpu.VMEM((12, 4 * c1, 4 * c1), BF16),
+            pltpu.SemaphoreType.DMA((6,)),
+            pltpu.SemaphoreType.DMA((5, len(DIRS))),
+            pltpu.SemaphoreType.DMA((5, len(DIRS))),
         ],
         compiler_params=pltpu.CompilerParams(
             collective_id=0, has_side_effects=True, vmem_limit_bytes=40 * 2**20
         ),
-    )(rows, base, encode, downward, middle_first, middle_second, up_w, skip_w, wide_w, head)
+    )(
+        cells, lift, encode_weight, downward_weight, middle_first, middle_second, up_w,
+        decode_weight, head,
+    )
     head_out = result[:, : 4 * comps].reshape(size_x, 2, 2, comps, yc, zc)
     head_out = jnp.transpose(head_out, (3, 0, 4, 1, 5, 2)).reshape(displacement.shape)
     return displacement.astype(F32) + head_out

time: 84.1 us -> 53.6 us (0.64)
  local copies, waits for them, and re-layouts: 31.4 us -> 7.27 us
  Pallas kernels: 32.9 us -> 45.3 us
  starting transfers between devices: 8.85 us -> 0 us
  other arithmetic: 7.94 us -> 0.74 us
  waiting for transfers between devices: 1.9 us -> 0 us
    slice x13 -> x0, local copies, waits for them, and re-layouts: 18.7 us -> none  [the longest x10 15.7 us: local(): cells[a:a + size_x + 2, b:b + size_y + 2]]
    pallas_call x1, Pallas kernels: 32.9 us -> 45.3 us  [local(): pl.pallas_call(functools.partial(unet, (comps, size_x, size_y, size_z, ro...]
    ppermute x6 -> x0, starting transfers between devices: 8.85 us -> none  [the longest x3 5.03 us: padded_by(): lax.ppermute(tail, axis, [(i, (i + 1) % count) for i in range(count)])]
    concatenate x4 -> x0, other arithmetic: 2.93 us -> none  [the longest x2 1.72 us: fine_kernel(): jnp.concatenate([jnp.concatenate([pair, blank], axis=1), jnp.concatenate(...]
    concatenate x2 -> x0, local copies, waits for them, and re-layouts: 2.04 us -> none  [the longest x1 2.03 us: local(): jnp.concatenate([cells[a:a + size_x + 2, b:b + size_y + 2] for a in range...]
    ppermute x6 -> x0, waiting for transfers between devices: 1.9 us -> none  [the longest x3 1.72 us: padded_by(): lax.ppermute(tail, axis, [(i, (i + 1) % count) for i in range(count)])]
    reshape x5 -> x1, local copies, waits for them, and re-layouts: 1.86 us -> 0.1 us  [local(): jnp.transpose(displacement, (1, 2, 3, 0)).reshape(size_x, size_y, -1)]
    slice x1 -> x0, other arithmetic: 1.6 us -> none  [padded_by(): lax.slice_in_dim(cells, cells.shape[dim] - width, cells.shape[dim], axis=...]
  transfers between devices with their start and end apart: 6 -> 0, of which waited for: 2 -> 0; matrix products, arithmetic and copies ran while one was open for 10% -> 0% of each run, Pallas kernels for 0% -> 0%
where the time goes in v1:
time: 53.6 us; the launch traced here: 53.4 us
  Pallas kernels  45.3 us (85%)
  local copies, waits for them, and re-layouts  7.27 us (14%)
  other arithmetic  0.74 us (1%)
    pallas_call x1, Pallas kernels, local(): pl.pallas_call(functools.partial(unet, (comps, size_x, size_y, size_z, ro...  45.3 us
    unnamed x16, local copies, waits for them, and re-layouts  4.96 us
    transpose x1, local copies, waits for them, and re-layouts, local(): jnp.transpose(head_out, (3, 0, 4, 1, 5, 2)).reshape(displacement.shape)  1.31 us

profile of v1, /device:TPU:0, one launch (start us, length us, event | category | flops | bytes accessed | tf_op | source)
XLA Modules:
  0.0 53.4 jit_solution(8180687765491331322)
XLA Ops:
  0.0 0.0 copy-start.5
  0.0 0.0 copy-start.1
  0.0 1.1 %copy.24 = bf16[27,64,3]{2,1,0:T(8,128)(2,1)S(1)} copy(bf16[27,64,3]{1,0,2:T(8,128)(2,1)} %param.10) | data formatting | bytes 20736 | tf_op args[1]
  1.1 0.0 copy-start
  1.1 0.1 pad.13.lift_ref
  1.3 1.1 %copy.25.downward_hbm = bf16[8,128,64]{2,1,0:T(8,128)(2,1)S(1)} copy(bf16[8,128,64]{1,2,0:T(8,128)(2,1)} %param.12) | data formatting | bytes 262144 | tf_op args[3]
  2.4 0.0 copy-done.5
  2.4 0.0 copy-start.4
  2.5 0.1 copy.23
  2.6 0.0 copy-start.6
  2.6 0.7 %copy-done.6 = bf16[3,64]{1,0:T(4,128)(2,1)S(1)} copy-done((bf16[3,64]{1,0:T(4,128)(2,1)S(1)}, bf16[3,64]{1,0:T(4,128)(2,1)}, u32[]{:S(2)}) %copy-start.6) | copy-done | bytes 408
  3.3 0.1 multiply_bitcast_fusion
  3.3 0.1 reshape.17
  3.4 0.0 copy-done.1
  3.4 0.0 copy-done
  3.4 0.0 copy-done.4
  3.5 0.0 copy-start.2
  3.5 1.0 %copy-done.2 = bf16[27,64,64]{2,1,0:T(8,128)(2,1)S(1)} copy-done((bf16[27,64,64]{2,1,0:T(8,128)(2,1)S(1)}, bf16[27,64,64]{2,1,0:T(8,128)(2,1)}, u32[]{:S(2)}) %copy-start.2) | copy-done | bytes 221208
  4.5 1.0 %copy-done.3 = bf16[27,64,128]{2,1,0:T(8,128)(2,1)S(1)} copy-done((bf16[27,64,128]{2,1,0:T(8,128)(2,1)S(1)}, bf16[27,64,128]{2,1,0:T(8,128)(2,1)}, u32[]{:S(2)}) %copy-start.3) | copy-done | bytes 442392
  5.5 45.3 %shard_map.91 = f32[4,16,128]{2,1,0:T(8,128)S(1)} custom-call(bf16[4,32,128]{2,1,0:T(8,128)(2,1)S(1)} %pad.12.cells_ref, bf16[27,64,128]{2,1,0:T(8,128)(2,1)S(1)} %pad.13.lift_ref, bf16[27,64,64]{2,1,0:T(8,128)(2,1)S(1)} %copy-done.2, bf16[8,128,64]{2,1,0:T(8,128)(2,1)S(1)} %copy.25.downward_hbm, bf16[27,128,128]{2,1,0:T(8,128)(2,1)S(1)} %copy-done, ...), custom_call_target="tpu_custom_call" | custom-call | tf_op jit(solution)/shard_map/pallas_call | solution.py:413
  50.8 0.2 reshape.18
  51.0 1.3 %copy.27 = f32[3,4,16,2,8,2]{1,5,4,3,2,0:T(2,128)S(1)} copy(f32[3,4,16,2,8,2]{4,2,1,0,5,3:T(8,128)S(1)} %bitcast.13) | data formatting | bytes 49152 | tf_op jit(solution)/shard_map/transpose | solution.py:454
  52.3 0.4 copy.28
  52.7 0.7 %convert_add_fusion = f32[3,4,32,16]{2,3,1,0:T(8,128)} fusion(f32[3,4,32,16]{2,3,1,0:T(8,128)S(1)} %copy.28, bf16[3,4,32,16]{2,3,1,0:T(8,128)(2,1)S(1)} %copy-done.5), kind=kLoop, calls=%fused_computation | loop fusion | flops 12288 | bytes 61440 | tf_op jit(solution)/shard_map/add | solution.py:455
  (6 shorter events, 0.1 us)
Async XLA Ops:
  0.0 2.4 %copy-start.5 = (bf16[3,4,32,16]{2,3,1,0:T(8,128)(2,1)S(1)}, bf16[3,4,32,16]{2,3,1,0:T(8,128)(2,1)}, u32[]{:S(2)}) copy-start(bf16[3,4,32,16]{2,3,1,0:T(8,128)(2,1)} %param.9) | copy-start | bytes 36868
  0.0 3.4 %copy-start.1 = (bf16[27,128,128]{2,1,0:T(8,128)(2,1)S(1)}, bf16[27,128,128]{2,1,0:T(8,128)(2,1)}, u32[]{:S(2)}) copy-start(bf16[27,128,128]{2,1,0:T(8,128)(2,1)} %second_hbm.1) | copy-start | bytes 2654212
  1.1 2.3 %copy-start = (bf16[27,128,128]{2,1,0:T(8,128)(2,1)S(1)}, bf16[27,128,128]{2,1,0:T(8,128)(2,1)}, u32[]{:S(2)}) copy-start(bf16[27,128,128]{2,1,0:T(8,128)(2,1)} %first_hbm.1) | copy-start | bytes 2654212
  2.4 1.0 %copy-start.4 = (bf16[8,64,128]{2,1,0:T(8,128)(2,1)S(1)}, bf16[8,64,128]{2,1,0:T(8,128)(2,1)}, u32[]{:S(2)}) copy-start(bf16[8,64,128]{2,1,0:T(8,128)(2,1)} %param.15) | copy-start | bytes 393220
  2.6 0.7 %copy-start.6 = (bf16[3,64]{1,0:T(4,128)(2,1)S(1)}, bf16[3,64]{1,0:T(4,128)(2,1)}, u32[]{:S(2)}) copy-start(bf16[3,64]{1,0:T(4,128)(2,1)} %param.17) | copy-start | bytes 1156
  3.5 1.0 %copy-start.2 = (bf16[27,64,64]{2,1,0:T(8,128)(2,1)S(1)}, bf16[27,64,64]{2,1,0:T(8,128)(2,1)}, u32[]{:S(2)}) copy-start(bf16[27,64,64]{2,1,0:T(8,128)(2,1)} %encode_hbm.1) | copy-start | bytes 663556
  4.5 1.0 %copy-start.3 = (bf16[27,64,128]{2,1,0:T(8,128)(2,1)S(1)}, bf16[27,64,128]{2,1,0:T(8,128)(2,1)}, u32[]{:S(2)}) copy-start(bf16[27,64,128]{2,1,0:T(8,128)(2,1)} %decode_hbm.1) | copy-start | bytes 1327108

commit v2 on v1

--- a/solution.py
+++ b/solution.py
@@ -15,7 +15,7 @@
     if (dx, dy, dz) != (0, 0, 0)
 ]
 F32, BF16 = jnp.float32, jnp.bfloat16
-RIM = 16
+RIM = 8
 
 
 def leaky(value):
@@ -38,7 +38,7 @@
 
 
 def exchange(body, below, above, first, last, sends, recvs, zc):
-    size_x, size_y = body.shape[0] - 2, body.shape[1] // zc - 2
+    size_x, size_y = body.shape[0] - 2, body.shape[1] - 2
     copies = []
     for number, (dx, dy, dz) in enumerate(DIRS):
         def span(step, size, offset):
@@ -49,8 +49,8 @@
         if dz == 0:
             sx, nx, tx = span(dx, size_x, 1)
             sy, ny, ty = span(dy, size_y, 1)
-            src = body.at[pl.ds(sx, nx), pl.ds(sy * zc, ny * zc)]
-            dst = body.at[pl.ds(tx, nx), pl.ds(ty * zc, ny * zc)]
+            src = body.at[pl.ds(sx, nx), pl.ds(sy, ny)]
+            dst = body.at[pl.ds(tx, nx), pl.ds(ty, ny)]
         else:
             sx, nx, tx = span(dx, size_x, 0)
             sy, ny, ty = span(dy, size_y, 0)
@@ -67,19 +67,21 @@
     return copies
 
 
-def send_cells(cells, block, sends, recvs):
-    size_x, size_y = cells.shape[:2]
+def send_cells(block, before, after, first, last, sends, recvs):
+    size_x, size_y = block.shape[0] - 4, block.shape[1] - 2
     copies = []
     for number, (dx, dy, dz) in enumerate(DIRS):
-        sx, nx, tx = {0: (0, size_x, 2), 1: (size_x - 2, 2, 0), -1: (0, 2, size_x + 2)}[dx]
-        sy, ny, ty = {
-            0: (0, size_y, RIM), 1: (size_y - RIM, RIM, 0), -1: (0, RIM, size_y + RIM)
-        }[dy]
+        sx, nx, tx = {0: (2, size_x, 2), 1: (size_x, 2, 0), -1: (2, 2, size_x + 2)}[dx]
+        sy, ny, ty = {0: (0, size_y, 1), 1: (size_y - 1, 1, 0), -1: (0, 1, size_y + 1)}[dy]
+        if dz == 0:
+            src = block.at[pl.ds(sx, nx), pl.ds(sy + 1, ny)]
+            dst = block.at[pl.ds(tx, nx), pl.ds(ty, ny)]
+        else:
+            src = (last if dz > 0 else first).at[pl.ds(sy, ny)]
+            dst = (before if dz > 0 else after).at[1 - dx, pl.ds(ty, ny)]
         copies.append(
             pltpu.make_async_remote_copy(
-                src_ref=cells.at[pl.ds(sx, nx), pl.ds(sy, ny)],
-                dst_ref=block.at[1 - dz, pl.ds(tx, nx), pl.ds(ty, ny)],
-                send_sem=sends.at[number], recv_sem=recvs.at[number],
+                src_ref=src, dst_ref=dst, send_sem=sends.at[number], recv_sem=recvs.at[number],
                 device_id=neighbour((dx, dy, dz)), device_id_type=MESH,
             )
         )
@@ -111,6 +113,10 @@
 
 def half_mask(rows):
     return lax.broadcasted_iota(jnp.int32, (rows, 128), 1) < 64
+
+
+def flat(plane):
+    return plane.astype(F32).reshape(plane.shape[0] * plane.shape[1], 128)
 
 
 def spread(edge, zc):
@@ -180,9 +186,9 @@
     cells_ref, lift_ref, encode_hbm, downward_hbm, first_hbm, second_hbm, up_hbm,
     decode_hbm, head_ref,
     out_ref,
-    block, joint, lhs32, lhs16, chunks, fp, fe, sp, se, up, ue, acc,
+    block, before, after, cell_first, cell_last, joint, lhs32, lhs16, chunks, fp, fe, sp, sf, se, up, ue, acc,
     s_below, s_above, s_first, s_last,
-    coarse_bufs, middle_bufs, deep_bufs, low, high,
+    coarse_bufs, middle_bufs, deep_bufs, low, middle, high,
     encode_raw, downward_raw, first_w, second_w, up_ref, decode_raw,
     encode_w, skip_w, wide_w,
     load_sems, send_sems, recv_sems,
@@ -203,9 +209,25 @@
     barrier = pltpu.get_barrier_semaphore()
     for direction in DIRS:
         pl.semaphore_signal(barrier, inc=1, device_id=neighbour(direction), device_id_type=MESH)
+    width, edge = comps * size_z, 2 * comps
+    own_rows = lax.broadcasted_iota(jnp.int32, (size_y, 128), 1)
+    rims = [None, None]
+    for x in range(size_x):
+        value = cells_ref[x].astype(F32)
+        block[x + 2, pl.ds(1, size_y // RIM)] = value.reshape(size_y // RIM, RIM, 128).astype(
+            BF16
+        )
+        for side, start in enumerate((0, width - edge)):
+            kept = jnp.where((own_rows >= start) & (own_rows < start + edge), value, 0.0)
+            shift = (edge * x - start) % 128
+            kept = pltpu.roll(kept, shift, 1) if shift else kept
+            rims[side] = kept if rims[side] is None else rims[side] + kept
+    cell_first[...] = rims[0].reshape(size_y // RIM, RIM, 128).astype(BF16)
+    cell_last[...] = rims[1].reshape(size_y // RIM, RIM, 128).astype(BF16)
     pl.semaphore_wait(barrier, len(DIRS))
-    cell_copies = send_cells(cells_ref, block, send_sems.at[4], recv_sems.at[4])
-    block[1, pl.ds(2, size_x), pl.ds(RIM, size_y), :] = cells_ref[...]
+    cell_copies = send_cells(
+        block, before, after, cell_first, cell_last, send_sems.at[4], recv_sems.at[4]
+    )
 
     groups = []
     for g in range(5):
@@ -226,18 +248,24 @@
     for copy in cell_copies:
         copy.wait_recv()
 
-    width = comps * size_z
-    edge = 2 * comps
     all_rows = size_y + 2 * RIM
     lane = lax.broadcasted_iota(jnp.int32, (all_rows, 128), 1)
+
+    def turned(value, shift):
+        return pltpu.roll(value, shift % 128, 1) if shift % 128 else value
+
     for x in range(size_x + 4):
-        own = pltpu.roll(block[1, x].astype(F32), edge, 1)
-        before = pltpu.roll(block[0, x].astype(F32), 128 - (width - edge), 1)
-        after = pltpu.roll(block[2, x].astype(F32), width + edge, 1)
+        near, place = (
+            (0, size_x - 2 + x) if x < 2 else (1, x - 2) if x < size_x + 2
+            else (2, x - size_x - 2)
+        )
+        own = turned(flat(block[x]), edge)
+        before_x = turned(flat(before[near]), -edge * place)
+        after_x = turned(flat(after[near]), width + edge - edge * place)
         joint[x] = jnp.where(
             lane < edge,
-            before,
-            jnp.where(lane < edge + width, own, jnp.where(lane < width + 2 * edge, after, 0.0)),
+            before_x,
+            jnp.where(lane < edge + width, own, jnp.where(lane < width + 2 * edge, after_x, 0.0)),
         )
     half = half_mask(rows_y)
     for x in range(size_x + 2):
@@ -289,11 +317,11 @@
             plane = jnp.stack(
                 [wide[:, :128].reshape(yc, zc, 128), wide[:, 128:].reshape(yc, zc, 128)], axis=1
             ).reshape(size_y, zc, 128)
-            sp[2 * x + g + 1, pl.ds(zc, size_y * zc), :] = plane.reshape(size_y * zc, 128)
+            sp[2 * x + g + 1, pl.ds(1, size_y)] = plane.astype(BF16)
             s_first[2 * x + g] = plane[:, 0:1, :]
             s_last[2 * x + g] = plane[:, zc - 1 : zc, :]
         coarse = rounded(coarse).astype(F32)
-        c_body[x + 1, pl.ds(zc, half_rows), :] = coarse
+        c_body[x + 1, pl.ds(1, yc)] = coarse.reshape(yc, zc, 128).astype(BF16)
         c_first[x] = coarse.reshape(yc, zc, 128)[:, 0:1, :]
         c_last[x] = coarse.reshape(yc, zc, 128)[:, zc - 1 : zc, :]
 
@@ -305,14 +333,15 @@
     def coarse_layer(bufs, weight, result):
         body, below, above = bufs[:3]
         for x in range(xc + 2):
-            down, upper = shifted(body[x], spread(below[x], zc), spread(above[x], zc), zc)
+            middle[x] = flat(body[x])
+            down, upper = shifted(middle[x], spread(below[x], zc), spread(above[x], zc), zc)
             low[x] = down
             high[x] = upper
-        value = rounded(coarse_conv(body, low, high, weight, zc)).astype(F32)
+        value = rounded(coarse_conv(middle, low, high, weight, zc)).astype(F32)
         target, _, _, first, last = result
         for x in range(xc):
             part = value[x * yc * zc : (x + 1) * yc * zc]
-            target[x + 1, pl.ds(zc, yc * zc), :] = part
+            target[x + 1, pl.ds(1, yc)] = part.reshape(yc, zc, 128).astype(BF16)
             first[x] = part.reshape(yc, zc, 128)[:, 0:1, :]
             last[x] = part.reshape(yc, zc, 128)[:, zc - 1 : zc, :]
 
@@ -338,14 +367,15 @@
 
     @pl.loop(0, size_x + 2)
     def _(x):
-        down, upper = shifted(sp[x], spread(s_below[x], zc), spread(s_above[x], zc), zc)
+        sf[x] = flat(sp[x])
+        down, upper = shifted(sf[x], spread(s_below[x], zc), spread(s_above[x], zc), zc)
         se[x] = jnp.where(fine_half, upper, down)
 
     loads[5].wait()
 
     @pl.loop(0, xc)
     def _(x):
-        acc[x] = fine_conv(sp, se, skip_w, 2 * x, 2, size_y, zc)
+        acc[x] = fine_conv(sf, se, skip_w, 2 * x, 2, size_y, zc)
 
     for copy in deep_copies:
         copy.wait_recv()
@@ -363,7 +393,7 @@
         edge_rows = jnp.where(
             coarse_end, spread(d_above[source], zc), spread(d_below[source], zc)
         )
-        plane = interleaved(rounded(dot(d_body[source].astype(BF16), kernel)).astype(F32))
+        plane = interleaved(rounded(dot(flat(d_body[source]).astype(BF16), kernel)).astype(F32))
         edge = interleaved(rounded(dot(edge_rows.astype(BF16), kernel)).astype(F32))
         down, upper = shifted(plane, edge, edge, zc)
         up[x] = plane
@@ -387,7 +417,7 @@
     comps, size_x, size_y, size_z = displacement.shape
     c1, c2 = encode_weight.shape[1], middle_first.shape[1]
     xc, yc, zc = size_x // 2, size_y // 2, size_z // 2
-    rows_y = -(-(size_y + 2) // 8) * 8
+    rows_y = size_y + 8
 
     cells = jnp.transpose(displacement, (1, 2, 3, 0)).reshape(size_x, size_y, -1)
     cells = jnp.pad(cells, ((0, 0), (0, 0), (0, 128 - cells.shape[-1])))
@@ -400,7 +430,7 @@
 
     def coarse_set():
         return [
-            pltpu.VMEM((xc + 2, (yc + 2) * zc, 128), F32),
+            pltpu.VMEM((xc + 2, yc + 2, zc, 128), BF16),
             pltpu.VMEM((xc + 2, yc + 2, 1, 128), F32),
             pltpu.VMEM((xc + 2, yc + 2, 1, 128), F32),
             pltpu.VMEM((xc, yc, 1, 128), F32),
@@ -416,18 +446,25 @@
         in_specs=[vmem, vmem] + [anywhere] * 6 + [vmem],
         out_specs=vmem,
         scratch_shapes=[
-            pltpu.VMEM((3, size_x + 4, size_y + 2 * RIM, 128), BF16),
+            pltpu.VMEM((size_x + 4, size_y // RIM + 2, RIM, 128), BF16),
+            pltpu.VMEM((3, size_y // RIM + 2, RIM, 128), BF16),
+            pltpu.VMEM((3, size_y // RIM + 2, RIM, 128), BF16),
+            pltpu.VMEM((size_y // RIM, RIM, 128), BF16),
+            pltpu.VMEM((size_y // RIM, RIM, 128), BF16),
             pltpu.VMEM((size_x + 4, size_y + 2 * RIM, 128), F32),
             pltpu.VMEM(((size_x + 2) * rows_y, 640), F32),
             pltpu.VMEM(((size_x + 2) * rows_y, 640), BF16),
             pltpu.VMEM((zc + 1, (size_x + 2) * rows_y, 128), F32),
-            first, first, fine, fine, fine, fine,
+            first, first,
+            pltpu.VMEM((size_x + 2, size_y + 2, zc, 128), BF16),
+            fine, fine, fine, fine,
             pltpu.VMEM((xc, 2 * yc * zc, 4 * c1), F32),
             pltpu.VMEM((size_x + 2, size_y + 2, 1, 128), F32),
             pltpu.VMEM((size_x + 2, size_y + 2, 1, 128), F32),
             pltpu.VMEM((size_x, size_y, 1, 128), F32),
             pltpu.VMEM((size_x, size_y, 1, 128), F32),
             coarse_set(), coarse_set(), coarse_set(),
+            pltpu.VMEM((xc + 2, (yc + 2) * zc, 128), F32),
             pltpu.VMEM((xc + 2, (yc + 2) * zc, 128), F32),
             pltpu.VMEM((xc + 2, (yc + 2) * zc, 128), F32),
             pltpu.VMEM(encode_weight.shape, BF16),
@@ -444,7 +481,7 @@
             pltpu.SemaphoreType.DMA((5, len(DIRS))),
         ],
         compiler_params=pltpu.CompilerParams(
-            collective_id=0, has_side_effects=True, vmem_limit_bytes=40 * 2**20
+            collective_id=0, has_side_effects=True, vmem_limit_bytes=63 * 2**20
         ),
     )(
         cells, lift, encode_weight, downward_weight, middle_first, middle_second, up_w,

time: 53.6 us -> 44.7 us (0.83)
  Pallas kernels: 45.3 us -> 36 us
    pallas_call x1, Pallas kernels: 45.3 us -> 36 us  [local(): pl.pallas_call(functools.partial(unet, (comps, size_x, size_y, size_z, ro...]
    unnamed x16 -> x8, local copies, waits for them, and re-layouts: 4.96 us -> 2.6 us
    slice x1, local copies, waits for them, and re-layouts: 0.01 us -> 0.77 us  [local(): head_out = result[:, :4 * comps].reshape(size_x, 2, 2, comps, yc, zc)]
    pad x1, local copies, waits for them, and re-layouts: 0.11 us -> 0.87 us  [local(): lift = jnp.pad(lift_weight, ((0, 0), (0, 0), (0, 128 - comps)))]
    pad x1, local copies, waits for them, and re-layouts: 0.01 us -> 0.63 us  [local(): cells = jnp.pad(cells, ((0, 0), (0, 0), (0, 128 - cells.shape[-1])))]
    pad x1, local copies, waits for them, and re-layouts: 0.01 us -> 0.6 us  [local(): head = jnp.pad(head, ((0, 16 - 4 * comps), (0, 0)))]
where the time goes in v2:
time: 44.7 us; the launch traced here: 44.4 us
  Pallas kernels  36 us (81%)
  local copies, waits for them, and re-layouts  7.63 us (17%)
  other arithmetic  0.74 us (2%)
    pallas_call x1, Pallas kernels, local(): pl.pallas_call(functools.partial(unet, (comps, size_x, size_y, size_z, ro...  36 us
    unnamed x8, local copies, waits for them, and re-layouts  2.6 us
    transpose x1, local copies, waits for them, and re-layouts, local(): jnp.transpose(head_out, (3, 0, 4, 1, 5, 2)).reshape(displacement.shape)  1.31 us

profile of v2, /device:TPU:0, one launch (start us, length us, event | category | flops | bytes accessed | tf_op | source)
XLA Modules:
  0.0 44.4 jit_solution(6824697392985054800)
XLA Ops:
  0.0 1.0 %copy.24 = bf16[27,64,3]{2,1,0:T(8,128)(2,1)S(1)} copy(bf16[27,64,3]{1,0,2:T(8,128)(2,1)} %param.10) | data formatting | bytes 20736 | tf_op args[1]
  1.0 0.0 copy-start.1
  1.1 0.9 %pad.13.lift_ref = bf16[27,64,128]{2,1,0:T(8,128)(2,1)} pad(bf16[27,64,3]{2,1,0:T(8,128)(2,1)S(1)} %copy.24, bf16[]{:T(256)} %constant.2.clone.1), padding=0_0x0_0x0_125 | pad | bytes 452738 | tf_op jit(solution)/shard_map/jit(_pad)/pad | solution.py:424
  1.9 0.0 copy-done.1
  2.0 0.0 copy-start
  2.0 0.8 %copy.25.downward_hbm = bf16[8,128,64]{2,1,0:T(8,128)(2,1)} copy(bf16[8,128,64]{1,2,0:T(8,128)(2,1)S(1)} %copy-done.1) | data formatting | bytes 262144 | tf_op args[3]
  2.8 0.0 copy-done
  2.8 0.1 copy.23
  2.9 0.6 %pad.12.cells_ref = bf16[4,32,128]{2,1,0:T(8,128)(2,1)} pad(bf16[4,32,48]{2,1,0:T(8,128)(2,1)S(1)} %copy.23, bf16[]{:T(256)} %constant.2.clone.1), padding=0_0x0_0x0_80 | pad | bytes 45058 | tf_op jit(solution)/shard_map/jit(_pad)/pad | solution.py:423
  3.6 0.0 copy-start.2
  3.6 0.7 %copy-done.2 = bf16[3,64]{1,0:T(4,128)(2,1)S(1)} copy-done((bf16[3,64]{1,0:T(4,128)(2,1)S(1)}, bf16[3,64]{1,0:T(4,128)(2,1)}, u32[]{:S(2)}) %copy-start.2) | copy-done | bytes 408
  4.2 0.1 multiply_bitcast_fusion
  4.3 0.1 reshape.17
  4.4 0.6 %pad.14.head_ref = bf16[16,256]{1,0:T(8,128)(2,1)} pad(bf16[12,256]{1,0:T(8,128)(2,1)S(1)} %reshape.17, bf16[]{:T(256)} %constant.2.clone.1), padding=0_4x0_0 | pad | bytes 14338 | tf_op jit(solution)/shard_map/jit(_pad)/pad | solution.py:429
  5.0 36.0 %shard_map.91 = f32[4,16,128]{2,1,0:T(8,128)} custom-call(bf16[4,32,128]{2,1,0:T(8,128)(2,1)} %pad.12.cells_ref, bf16[27,64,128]{2,1,0:T(8,128)(2,1)} %pad.13.lift_ref, bf16[27,64,64]{2,1,0:T(8,128)(2,1)} %encode_hbm.1, bf16[8,128,64]{2,1,0:T(8,128)(2,1)} %copy.25.downward_hbm, bf16[27,128,128]{2,1,0:T(8,128)(2,1)} %first_hbm.1, ...), custom_call_target="tpu_custom_call" | custom-call | tf_op jit(solution)/shard_map/pallas_call | solution.py:443
  41.0 0.8 %copy.26 = f32[4,12,128]{2,0,1:T(4,128)S(1)} copy(f32[4,12,128]{2,1,0:T(8,128)} %bitcast.15) | data formatting | bytes 49152 | tf_op jit(solution)/shard_map/slice | solution.py:490
  41.8 0.2 reshape.18
  42.0 1.3 %copy.27 = f32[3,4,16,2,8,2]{1,5,4,3,2,0:T(2,128)S(1)} copy(f32[3,4,16,2,8,2]{4,2,1,0,5,3:T(8,128)S(1)} %bitcast.11) | data formatting | bytes 49152 | tf_op jit(solution)/shard_map/transpose | solution.py:491
  43.3 0.4 copy.28
  43.8 0.7 %convert_add_fusion = f32[3,4,32,16]{2,3,1,0:T(8,128)} fusion(f32[3,4,32,16]{2,3,1,0:T(8,128)S(1)} %copy.28, bf16[3,4,32,16]{2,3,1,0:T(8,128)(2,1)S(1)} %copy-done), kind=kLoop, calls=%fused_computation | loop fusion | flops 12288 | bytes 61440 | tf_op jit(solution)/shard_map/add | solution.py:492
  (2 shorter events, 0.0 us)
Async XLA Ops:
  1.0 0.9 %copy-start.1 = (bf16[8,128,64]{1,2,0:T(8,128)(2,1)S(1)}, bf16[8,128,64]{1,2,0:T(8,128)(2,1)}, u32[]{:S(2)}) copy-start(bf16[8,128,64]{1,2,0:T(8,128)(2,1)} %param.12) | copy-start | bytes 393220
  2.0 0.9 %copy-start = (bf16[3,4,32,16]{2,3,1,0:T(8,128)(2,1)S(1)}, bf16[3,4,32,16]{2,3,1,0:T(8,128)(2,1)}, u32[]{:S(2)}) copy-start(bf16[3,4,32,16]{2,3,1,0:T(8,128)(2,1)} %param.9) | copy-start | bytes 36868
  3.6 0.7 %copy-start.2 = (bf16[3,64]{1,0:T(4,128)(2,1)S(1)}, bf16[3,64]{1,0:T(4,128)(2,1)}, u32[]{:S(2)}) copy-start(bf16[3,64]{1,0:T(4,128)(2,1)} %param.17) | copy-start | bytes 1156

commit v3 on v2

--- a/solution.py
+++ b/solution.py
@@ -62,9 +62,12 @@
                 device_id=neighbour((dx, dy, dz)), device_id_type=MESH,
             )
         )
+    return copies
+
+
+def launch(copies):
     for copy in copies:
         copy.start()
-    return copies
 
 
 def send_cells(block, before, after, first, last, sends, recvs):
@@ -235,6 +238,8 @@
         for tap in range(2 * g, min(2 * g + 2, 9)):
             for c in range(3):
                 piece = lift_ref[3 * tap + c].astype(F32)
+                blank = jnp.zeros((piece.shape[0], 128 - comps), F32)
+                piece = jnp.concatenate([piece, blank], axis=1)
                 shift = 64 * (tap % 2) + comps * c
                 piece = pltpu.roll(piece, shift, 1) if shift else piece
                 total = piece if total is None else total + piece
@@ -326,9 +331,12 @@
         c_last[x] = coarse.reshape(yc, zc, 128)[:, zc - 1 : zc, :]
 
     coarse_copies = exchange(*coarse_bufs, send_sems.at[0], recv_sems.at[0], zc)
+    launch(coarse_copies)
     skip_copies = exchange(
         sp, s_below, s_above, s_first, s_last, send_sems.at[1], recv_sems.at[1], zc
     )
+
+    launch([c for c, d in zip(skip_copies, DIRS) if d[0] == 0])
 
     def coarse_layer(bufs, weight, result):
         body, below, above = bufs[:3]
@@ -354,12 +362,15 @@
         copy.wait_recv()
     coarse_layer(coarse_bufs, first_w, middle_bufs)
     middle_copies = exchange(*middle_bufs, send_sems.at[2], recv_sems.at[2], zc)
+    launch(middle_copies)
+    launch([c for c, d in zip(skip_copies, DIRS) if d[0] != 0])
 
     for copy in middle_copies:
         copy.wait_recv()
     loads[4].wait()
     coarse_layer(middle_bufs, second_w, deep_bufs)
     deep_copies = exchange(*deep_bufs, send_sems.at[3], recv_sems.at[3], zc)
+    launch(deep_copies)
 
     for copy in skip_copies:
         copy.wait_recv()
@@ -421,7 +432,6 @@
 
     cells = jnp.transpose(displacement, (1, 2, 3, 0)).reshape(size_x, size_y, -1)
     cells = jnp.pad(cells, ((0, 0), (0, 0), (0, 128 - cells.shape[-1])))
-    lift = jnp.pad(lift_weight, ((0, 0), (0, 0), (0, 128 - comps)))
     up_w = up_weight.reshape(4, 2 * c1, c2)
     head = jnp.einsum("pq,ki->pkqi", jnp.eye(4, dtype=BF16), head_weight).reshape(
         4 * comps, 4 * c1
@@ -484,7 +494,7 @@
             collective_id=0, has_side_effects=True, vmem_limit_bytes=63 * 2**20
         ),
     )(
-        cells, lift, encode_weight, downward_weight, middle_first, middle_second, up_w,
+        cells, lift_weight, encode_weight, downward_weight, middle_first, middle_second, up_w,
         decode_weight, head,
     )
     head_out = result[:, : 4 * comps].reshape(size_x, 2, 2, comps, yc, zc)

time: 44.7 us -> 44.2 us (0.989)
  local copies, waits for them, and re-layouts: 7.63 us -> 6.04 us
  other arithmetic: 0.74 us -> 1.43 us
  Pallas kernels: 36 us -> 36.5 us
    pad x1 -> x0, local copies, waits for them, and re-layouts: 0.87 us -> none  [local(): lift = jnp.pad(lift_weight, ((0, 0), (0, 0), (0, 128 - comps)))]
    unnamed x8, local copies, waits for them, and re-layouts: 2.6 us -> 1.88 us
    transpose x1, other arithmetic: 0.08 us -> 0.77 us  [local(): jnp.einsum('pq,ki->pkqi', jnp.eye(4, dtype=BF16), head_weight)]
    pallas_call x1, Pallas kernels: 36 us -> 36.5 us  [local(): pl.pallas_call(functools.partial(unet, (comps, size_x, size_y, size_z, ro...]
where the time goes in v3:
time: 44.2 us; the launch traced here: 44 us
  Pallas kernels  36.5 us (83%)
  local copies, waits for them, and re-layouts  6.04 us (14%)
  other arithmetic  1.43 us (3%)
    pallas_call x1, Pallas kernels, local(): pl.pallas_call(functools.partial(unet, (comps, size_x, size_y, size_z, ro...  36.5 us
    unnamed x8, local copies, waits for them, and re-layouts  1.88 us
    transpose x1, local copies, waits for them, and re-layouts, local(): jnp.transpose(head_out, (3, 0, 4, 1, 5, 2)).reshape(displacement.shape)  1.31 us

profile of v3, /device:TPU:0, one launch (start us, length us, event | category | flops | bytes accessed | tf_op | source)
XLA Modules:
  0.0 44.0 jit_solution(6105326157567166758)
XLA Ops:
  0.0 0.0 copy-start
  0.0 0.8 %multiply_bitcast_fusion = bf16[4,3,4,64]{3,2,1,0:T(4,128)(2,1)S(1)} fusion(bf16[3,64]{1,0:T(4,128)(2,1)} %param.17, bf16[4,4]{1,0:T(4,128)(2,1)S(1)} %fusion), kind=kLoop, calls=%fused_computation.1 | loop fusion | flops 3072 | bytes 6560 | tf_op jit(solution)/shard_map/pq,ki->pkqi/transpose | solution.py:436
  0.8 0.1 reshape.17
  0.9 0.0 copy-start.1
  0.9 0.6 %pad.9.head_ref = bf16[16,256]{1,0:T(8,128)(2,1)} pad(bf16[12,256]{1,0:T(8,128)(2,1)S(1)} %reshape.17, bf16[]{:T(256)} %constant.2.clone.1), padding=0_4x0_0 | pad | bytes 14338 | tf_op jit(solution)/shard_map/jit(_pad)/pad | solution.py:439
  1.5 0.0 copy-done
  1.5 0.1 copy.23
  1.6 0.6 %pad.8.cells_ref = bf16[4,32,128]{2,1,0:T(8,128)(2,1)} pad(bf16[4,32,48]{2,1,0:T(8,128)(2,1)S(1)} %copy.23, bf16[]{:T(256)} %constant.2.clone.1), padding=0_0x0_0x0_80 | pad | bytes 45058 | tf_op jit(solution)/shard_map/jit(_pad)/pad | solution.py:434
  2.2 0.0 copy-done.1
  2.2 0.0 copy-start.2
  2.2 0.8 %copy.25.downward_hbm = bf16[8,128,64]{2,1,0:T(8,128)(2,1)} copy(bf16[8,128,64]{1,2,0:T(8,128)(2,1)S(1)} %copy-done.1) | data formatting | bytes 262144 | tf_op args[3]
  3.1 0.0 copy-done.2
  3.1 1.0 %copy.24.lift_ref = bf16[27,64,3]{2,1,0:T(8,128)(2,1)} copy(bf16[27,64,3]{1,0,2:T(8,128)(2,1)S(1)} %copy-done.2) | data formatting | bytes 20736 | tf_op args[1]
  4.1 36.5 %shard_map.91 = f32[4,16,128]{2,1,0:T(8,128)} custom-call(bf16[4,32,128]{2,1,0:T(8,128)(2,1)} %pad.8.cells_ref, bf16[27,64,3]{2,1,0:T(8,128)(2,1)} %copy.24.lift_ref, bf16[27,64,64]{2,1,0:T(8,128)(2,1)} %encode_hbm.1, bf16[8,128,64]{2,1,0:T(8,128)(2,1)} %copy.25.downward_hbm, bf16[27,128,128]{2,1,0:T(8,128)(2,1)} %first_hbm.1, ...), custom_call_target="tpu_custom_call" | custom-call | tf_op jit(solution)/shard_map/pallas_call | solution.py:453
  40.6 0.8 %copy.26 = f32[4,12,128]{2,0,1:T(4,128)S(1)} copy(f32[4,12,128]{2,1,0:T(8,128)} %bitcast.15) | data formatting | bytes 49152 | tf_op jit(solution)/shard_map/slice | solution.py:500
  41.4 0.2 reshape.18
  41.6 1.3 %copy.27 = f32[3,4,16,2,8,2]{1,5,4,3,2,0:T(2,128)S(1)} copy(f32[3,4,16,2,8,2]{4,2,1,0,5,3:T(8,128)S(1)} %bitcast.11) | data formatting | bytes 49152 | tf_op jit(solution)/shard_map/transpose | solution.py:501
  42.9 0.4 copy.28
  43.3 0.7 %convert_add_fusion = f32[3,4,32,16]{2,3,1,0:T(8,128)} fusion(f32[3,4,32,16]{2,3,1,0:T(8,128)S(1)} %copy.28, bf16[3,4,32,16]{2,3,1,0:T(8,128)(2,1)S(1)} %copy-done), kind=kLoop, calls=%fused_computation | loop fusion | flops 12288 | bytes 61440 | tf_op jit(solution)/shard_map/add | solution.py:502
  (2 shorter events, 0.0 us)
Async XLA Ops:
  0.0 1.5 %copy-start = (bf16[3,4,32,16]{2,3,1,0:T(8,128)(2,1)S(1)}, bf16[3,4,32,16]{2,3,1,0:T(8,128)(2,1)}, u32[]{:S(2)}) copy-start(bf16[3,4,32,16]{2,3,1,0:T(8,128)(2,1)} %param.9) | copy-start | bytes 36868
  0.9 1.4 %copy-start.1 = (bf16[8,128,64]{1,2,0:T(8,128)(2,1)S(1)}, bf16[8,128,64]{1,2,0:T(8,128)(2,1)}, u32[]{:S(2)}) copy-start(bf16[8,128,64]{1,2,0:T(8,128)(2,1)} %param.12) | copy-start | bytes 393220
  2.2 0.9 %copy-start.2 = (bf16[27,64,3]{1,0,2:T(8,128)(2,1)S(1)}, bf16[27,64,3]{1,0,2:T(8,128)(2,1)}, u32[]{:S(2)}) copy-start(bf16[27,64,3]{1,0,2:T(8,128)(2,1)} %param.10) | copy-start | bytes 31108
